TPU v7x, 32 devices: a whole 2x2x4 slice. The times are simulated.
32 devices in a mesh: dp: 2 (over x), pipe: 4 (over z), mp: 4 (over y, core).
Axes of the slice: x: 2, y: 2, z: 4, core: 2. Of those that a mesh axis runs over, the one named last changes fastest.
Arguments:
- inputs: bfloat16 [4, 128, 1024], P(None, 'dp', 'mp'), may hold values from -6 to 6
- cotangent: bfloat16 [4, 128, 1024], P(None, 'dp', 'mp'), may hold values from -6 to 6
- gain: float32 [4, 1024], P('pipe'), may hold values from 0.25 to 1.75
- weight_in: bfloat16 [4, 1024, 32768], P('pipe', None, 'mp'), may hold values from -0.1875 to 0.1875
- weight_out: bfloat16 [4, 32768, 1024], P('pipe', 'mp'), may hold values from -0.03125 to 0.03125
Outputs:
- grad_in: bfloat16 [4, 1024, 32768], P('pipe', 'dp', 'mp')
- grad_out: bfloat16 [4, 32768, 1024], P('pipe', 'mp', 'dp')
- grad_gain: float32 [4, 1024], P('pipe', 'mp')
All inputs are finite; a program needn't handle non-finite values.
Results may differ from a plain program's by a relative error of at most 0.023.
Values may be sent and summed in bfloat16 or wider, within the bound.
A program may use at most 128 MiB of HBM per device.

v0:
```python
import math

import jax
import jax.numpy as jnp
from jax import lax
from jax.sharding import PartitionSpec as P

GELU_COEF = math.sqrt(2.0 / math.pi)
CUBIC_COEF = 0.044715
NORM_EPS = 1e-06
CONTRACT_LAST = (((1,), (1,)), ((), ()))
CONTRACT_FIRST = (((0,), (0,)), ((), ()))


def shifted(shard, axis, by):
    count = lax.axis_size(axis)
    pairs = [(i, i + by) for i in range(count) if 0 <= i + by < count]
    return lax.ppermute(shard, axis, pairs)


def gelu_parts(values):
    tangent = jnp.tanh(GELU_COEF * (values + CUBIC_COEF * values * values * values))
    output = 0.5 * values * (1.0 + tangent)
    derivative = 0.5 * (1.0 + tangent) + 0.5 * values * (1.0 - tangent * tangent) * GELU_COEF * (
        1.0 + 3.0 * CUBIC_COEF * values * values
    )
    return (output, derivative)


def shards(inputs, cotangent, gain, weight_in, weight_out):
    segment_count = lax.axis_size("pipe")
    section = lax.axis_index("pipe")
    part_index = lax.axis_index("mp")
    replicas = lax.axis_size("dp")
    micro, row_count, width = inputs.shape
    weight_first = weight_in[0]
    weight_second = weight_out[0]
    gain_row = gain[0]
    full_width = gain_row.shape[0]
    hidden = weight_first.shape[1]
    gain_own = lax.dynamic_slice_in_dim(gain_row, part_index * width, width, 0)
    turns = segment_count + micro - 1

    def forward_turn(turn, carry):
        incoming, rows_save, scale_save, gate_save = carry
        micro_slot = turn - section
        is_active = (micro_slot >= 0) & (micro_slot < micro)
        slot_index = jnp.clip(micro_slot, 0, micro - 1)
        first_rows = lax.dynamic_index_in_dim(inputs, slot_index, 0, keepdims=False)
        segment_input = jnp.where(section == 0, first_rows, incoming)
        whole_rows = lax.all_gather(segment_input, "mp", axis=1, tiled=True)

        def forward_active(operands):
            gathered, rows_keep, scale_keep, gate_keep = operands
            values = gathered.astype(jnp.float32)
            inv_rms = lax.rsqrt(jnp.mean(values * values, axis=1) + NORM_EPS)
            normed = (values * inv_rms[:, None] * gain_row).astype(jnp.bfloat16)
            gate_input = jnp.dot(normed, weight_first, preferred_element_type=jnp.float32)
            activated = gelu_parts(gate_input)[0].astype(jnp.bfloat16)
            branch = jnp.dot(activated, weight_second, preferred_element_type=jnp.float32)
            rows_keep = lax.dynamic_update_index_in_dim(rows_keep, gathered, slot_index, 0)
            scale_keep = lax.dynamic_update_index_in_dim(scale_keep, inv_rms, slot_index, 0)
            gate_keep = lax.dynamic_update_index_in_dim(gate_keep, gate_input, slot_index, 0)
            return (branch, rows_keep, scale_keep, gate_keep)

        def forward_resting(operands):
            gathered, rows_keep, scale_keep, gate_keep = operands
            return (
                jnp.zeros((row_count, full_width), jnp.float32),
                rows_keep,
                scale_keep,
                gate_keep,
            )

        branch, rows_save, scale_save, gate_save = lax.cond(
            is_active,
            forward_active,
            forward_resting,
            (whole_rows, rows_save, scale_save, gate_save),
        )
        branch_sum = lax.psum_scatter(branch, "mp", scatter_dimension=1, tiled=True)
        result = (segment_input.astype(jnp.float32) + branch_sum).astype(jnp.bfloat16)
        passed = shifted(result, "pipe", 1)
        return (passed, rows_save, scale_save, gate_save)

    forward_init = (
        jnp.zeros((row_count, width), jnp.bfloat16),
        jnp.zeros((micro, row_count, full_width), jnp.bfloat16),
        jnp.zeros((micro, row_count), jnp.float32),
        jnp.zeros((micro, row_count, hidden), jnp.float32),
    )
    forward_out = lax.fori_loop(0, turns, forward_turn, forward_init)
    rows_save = forward_out[1]
    scale_save = forward_out[2]
    gate_save = forward_out[3]

    def backward_turn(turn, carry):
        incoming, pregrad_save, outgrad_save, gain_acc = carry
        micro_slot = turn - (segment_count - 1 - section)
        is_active = (micro_slot >= 0) & (micro_slot < micro)
        slot_index = jnp.clip(micro_slot, 0, micro - 1)
        last_rows = lax.dynamic_index_in_dim(cotangent, slot_index, 0, keepdims=False).astype(
            jnp.float32
        )
        grad_rows = jnp.where(section == segment_count - 1, last_rows, incoming)
        whole_grad = lax.all_gather(grad_rows.astype(jnp.bfloat16), "mp", axis=1, tiled=True)

        def backward_active(operands):
            gathered, pregrad_keep, outgrad_keep = operands
            gate_input = lax.dynamic_index_in_dim(gate_save, slot_index, 0, keepdims=False)
            slopes = gelu_parts(gate_input)[1]
            inner_grad = lax.dot_general(
                gathered, weight_second, CONTRACT_LAST, preferred_element_type=jnp.float32
            )
            pre_grad = (inner_grad * slopes).astype(jnp.bfloat16)
            norm_part = lax.dot_general(
                pre_grad, weight_first, CONTRACT_LAST, preferred_element_type=jnp.float32
            )
            pregrad_keep = lax.dynamic_update_index_in_dim(pregrad_keep, pre_grad, slot_index, 0)
            outgrad_keep = lax.dynamic_update_index_in_dim(outgrad_keep, gathered, slot_index, 0)
            return (norm_part, pregrad_keep, outgrad_keep)

        def backward_resting(operands):
            gathered, pregrad_keep, outgrad_keep = operands
            return (jnp.zeros((row_count, full_width), jnp.float32), pregrad_keep, outgrad_keep)

        norm_part, pregrad_save, outgrad_save = lax.cond(
            is_active, backward_active, backward_resting, (whole_grad, pregrad_save, outgrad_save)
        )
        values = lax.dynamic_index_in_dim(rows_save, slot_index, 0, keepdims=False).astype(
            jnp.float32
        )
        inv_rms = lax.dynamic_index_in_dim(scale_save, slot_index, 0, keepdims=False)
        unit_full = values * inv_rms[:, None]
        unit_own = lax.dynamic_slice_in_dim(unit_full, part_index * width, width, 1)
        norm_grad = lax.psum_scatter(norm_part, "mp", scatter_dimension=1, tiled=True)
        scaled = norm_grad * gain_own
        row_dot = lax.psum(jnp.sum(scaled * unit_own, axis=1), "mp")
        previous = grad_rows + inv_rms[:, None] * (
            scaled - unit_own * row_dot[:, None] / full_width
        )
        gain_acc = gain_acc + jnp.where(is_active, jnp.sum(norm_grad * unit_own, axis=0), 0.0)
        passed = shifted(previous, "pipe", -1)
        return (passed, pregrad_save, outgrad_save, gain_acc)

    backward_init = (
        jnp.zeros((row_count, width), jnp.float32),
        jnp.zeros((micro, row_count, hidden), jnp.bfloat16),
        jnp.zeros((micro, row_count, full_width), jnp.bfloat16),
        jnp.zeros((width,), jnp.float32),
    )
    backward_out = lax.fori_loop(0, turns, backward_turn, backward_init)
    all_rows = micro * row_count
    pregrad_all = backward_out[1].reshape(all_rows, hidden)
    outgrad_all = backward_out[2].reshape(all_rows, full_width)
    gain_acc = backward_out[3]
    normed_all = (
        (rows_save.astype(jnp.float32) * scale_save[:, :, None] * gain_row)
        .astype(jnp.bfloat16)
        .reshape(all_rows, full_width)
    )
    activated_all = gelu_parts(gate_save)[0].astype(jnp.bfloat16).reshape(all_rows, hidden)
    half_width = full_width // replicas
    packed = jnp.stack((normed_all, outgrad_all)).reshape(2, all_rows, replicas, half_width)
    swapped = lax.all_to_all(packed, "dp", split_axis=2, concat_axis=1, tiled=True)
    columns = swapped.reshape(2, replicas * all_rows, half_width)
    pregrad_piece = lax.all_gather(pregrad_all, "dp", axis=0, tiled=True)
    activated_piece = lax.all_gather(activated_all, "dp", axis=0, tiled=True)
    normed_cols = columns[0]
    outgrad_cols = columns[1]
    in_term = lax.dot_general(
        normed_cols, pregrad_piece, CONTRACT_FIRST, preferred_element_type=jnp.float32
    )
    out_term = lax.dot_general(
        outgrad_cols, activated_piece, CONTRACT_FIRST, preferred_element_type=jnp.float32
    )
    grad_sums = jnp.stack((in_term, out_term))
    in_part = grad_sums[0]
    out_part = grad_sums[1]
    grad_first = in_part.astype(jnp.bfloat16)[None]
    grad_second = out_part.astype(jnp.bfloat16).T[None]
    gain_total = lax.psum(gain_acc, "dp")[None]
    return (grad_first, grad_second, gain_total)


def solution(mesh):
    in_specs = (
        P(None, "dp", "mp"),
        P(None, "dp", "mp"),
        P("pipe", None),
        P("pipe", None, "mp"),
        P("pipe", "mp", None),
    )
    out_specs = (P("pipe", "dp", "mp"), P("pipe", "mp", "dp"), P("pipe", "mp"))
    return jax.shard_map(shards, mesh=mesh, in_specs=in_specs, out_specs=out_specs, check_vma=False)
```

profile of v0, /device:TPU:0, one launch (start us, length us, event | category | flops | bytes accessed | tf_op | source)
XLA Modules:
  0.0 1032.1 jit_solution(17084897989914273569)
XLA Ops:
  13.2 334.4 %while.42 = (s32[]{:T(128)}, bf16[64,256]{1,0:T(8,128)(2,1)S(1)}, bf16[4,64,1024]{2,1,0:T(8,128)(2,1)S(1)}, f32[4,64]{1,0:T(4,128)S(1)}, f32[4,64,8192]{2,1,0:T(...) while((s32[]{:T(128)}, bf16[64,256]{1,0:T(8,128)(2,1)S(1)}, ...), condition=%wide.region_5.6_spmd, body=%wide.region_0.5_spmd.sunk | while | flops 2152726528 | bytes 110303480 | solution.py:92
  14.0 6.5 all_gather.28
  20.5 14.5 %conditional.5 = (f32[64,1024]{1,0:T(8,128)S(1)}, bf16[4,64,1024]{2,1,0:T(8,128)(2,1)S(1)}, f32[4,64]{1,0:T(4,128)S(1)}, f32[4,64,8192]{2,1,0:T(8,128)}) conditional(s32[]{:T(128)} %convert_element_type.141, (bf16[4,64,1024]{2,1,0:T(8,128)(2,1)S(1)}, f32[4,64]{1,0:T(4,128)S(1)}, f32[4,64,8192]{2,1,0:T(8,128)}) %tuple.97, ...), branch_computations={%region_1.1_spmd, %region_2.3_spmd} | conditional | flops 2152660992 | bytes 107747168 | solution.py:75
  20.7 10.4 %bitcast_dynamic-update-slice_fusion = (f32[4,64,8192]{2,1,0:T(8,128)}, f32[64,8192]{1,0:T(8,128)S(1)}) fusion(f32[4,64,8192]{2,1,0:T(8,128)} %get-tuple-element.578, s32[]{:T(128)S(6)} %select_n.85, bf16[1024,8192]{1,0:T(8,128)(2,1)} %get-tuple-element.573, bf16[64,1024]{1,0:T(8,128)(2,1)S(1)} %get-tuple-element.571, f32[1024]{0:T(1024)S(1)} %bitcast.78, ...), kind=kOutput, calls=%fused_computation.6 | convolution fusion | flops 1074003968 | bytes 21106948 | tf_op jit(solution)/shard_map/while/body/eval_jaxpr/cond/branch_1_fun/dot_general | solution.py:58
  35.8 18.8 %reduce-scatter.3.cloned.1.call-done = f32[64,256]{1,0:T(8,128)} async-done(((f32[64,1024]{1,0:T(8,128)}), f32[64,256]{1,0:T(8,128)}) %reduce-scatter.3.cloned.1.call-update) | async-done | bytes 65552 | tf_op jit(solution)/shard_map/while/body/eval_jaxpr/reduce_scatter | solution.py:81
  61.2 5.4 all_gather.28
  66.6 14.5 %conditional.5 = (f32[64,1024]{1,0:T(8,128)S(1)}, bf16[4,64,1024]{2,1,0:T(8,128)(2,1)S(1)}, f32[4,64]{1,0:T(4,128)S(1)}, f32[4,64,8192]{2,1,0:T(8,128)}) conditional(s32[]{:T(128)} %convert_element_type.141, (bf16[4,64,1024]{2,1,0:T(8,128)(2,1)S(1)}, f32[4,64]{1,0:T(4,128)S(1)}, f32[4,64,8192]{2,1,0:T(8,128)}) %tuple.97, ...), branch_computations={%region_1.1_spmd, %region_2.3_spmd} | conditional | flops 2152660992 | bytes 107747168 | solution.py:75
  66.7 10.4 %bitcast_dynamic-update-slice_fusion = (f32[4,64,8192]{2,1,0:T(8,128)}, f32[64,8192]{1,0:T(8,128)S(1)}) fusion(f32[4,64,8192]{2,1,0:T(8,128)} %get-tuple-element.578, s32[]{:T(128)S(6)} %select_n.85, bf16[1024,8192]{1,0:T(8,128)(2,1)} %get-tuple-element.573, bf16[64,1024]{1,0:T(8,128)(2,1)S(1)} %get-tuple-element.571, f32[1024]{0:T(1024)S(1)} %bitcast.78, ...), kind=kOutput, calls=%fused_computation.6 | convolution fusion | flops 1074003968 | bytes 21106948 | tf_op jit(solution)/shard_map/while/body/eval_jaxpr/cond/branch_1_fun/dot_general | solution.py:58
  81.9 19.2 %reduce-scatter.3.cloned.1.call-done = f32[64,256]{1,0:T(8,128)} async-done(((f32[64,1024]{1,0:T(8,128)}), f32[64,256]{1,0:T(8,128)}) %reduce-scatter.3.cloned.1.call-update) | async-done | bytes 65552 | tf_op jit(solution)/shard_map/while/body/eval_jaxpr/reduce_scatter | solution.py:81
  107.7 5.4 all_gather.28
  113.1 14.5 %conditional.5 = (f32[64,1024]{1,0:T(8,128)S(1)}, bf16[4,64,1024]{2,1,0:T(8,128)(2,1)S(1)}, f32[4,64]{1,0:T(4,128)S(1)}, f32[4,64,8192]{2,1,0:T(8,128)}) conditional(s32[]{:T(128)} %convert_element_type.141, (bf16[4,64,1024]{2,1,0:T(8,128)(2,1)S(1)}, f32[4,64]{1,0:T(4,128)S(1)}, f32[4,64,8192]{2,1,0:T(8,128)}) %tuple.97, ...), branch_computations={%region_1.1_spmd, %region_2.3_spmd} | conditional | flops 2152660992 | bytes 107747168 | solution.py:75
  113.2 10.4 %bitcast_dynamic-update-slice_fusion = (f32[4,64,8192]{2,1,0:T(8,128)}, f32[64,8192]{1,0:T(8,128)S(1)}) fusion(f32[4,64,8192]{2,1,0:T(8,128)} %get-tuple-element.578, s32[]{:T(128)S(6)} %select_n.85, bf16[1024,8192]{1,0:T(8,128)(2,1)} %get-tuple-element.573, bf16[64,1024]{1,0:T(8,128)(2,1)S(1)} %get-tuple-element.571, f32[1024]{0:T(1024)S(1)} %bitcast.78, ...), kind=kOutput, calls=%fused_computation.6 | convolution fusion | flops 1074003968 | bytes 21106948 | tf_op jit(solution)/shard_map/while/body/eval_jaxpr/cond/branch_1_fun/dot_general | solution.py:58
  128.4 20.1 %reduce-scatter.3.cloned.1.call-done = f32[64,256]{1,0:T(8,128)} async-done(((f32[64,1024]{1,0:T(8,128)}), f32[64,256]{1,0:T(8,128)}) %reduce-scatter.3.cloned.1.call-update) | async-done | bytes 65552 | tf_op jit(solution)/shard_map/while/body/eval_jaxpr/reduce_scatter | solution.py:81
  155.1 5.4 all_gather.28
  160.5 14.6 %conditional.5 = (f32[64,1024]{1,0:T(8,128)S(1)}, bf16[4,64,1024]{2,1,0:T(8,128)(2,1)S(1)}, f32[4,64]{1,0:T(4,128)S(1)}, f32[4,64,8192]{2,1,0:T(8,128)}) conditional(s32[]{:T(128)} %convert_element_type.141, (bf16[4,64,1024]{2,1,0:T(8,128)(2,1)S(1)}, f32[4,64]{1,0:T(4,128)S(1)}, f32[4,64,8192]{2,1,0:T(8,128)}) %tuple.97, ...), branch_computations={%region_1.1_spmd, %region_2.3_spmd} | conditional | flops 2152660992 | bytes 107747168 | solution.py:75
  160.6 10.3 %bitcast_dynamic-update-slice_fusion = (f32[4,64,8192]{2,1,0:T(8,128)}, f32[64,8192]{1,0:T(8,128)S(1)}) fusion(f32[4,64,8192]{2,1,0:T(8,128)} %get-tuple-element.578, s32[]{:T(128)S(6)} %select_n.85, bf16[1024,8192]{1,0:T(8,128)(2,1)} %get-tuple-element.573, bf16[64,1024]{1,0:T(8,128)(2,1)S(1)} %get-tuple-element.571, f32[1024]{0:T(1024)S(1)} %bitcast.78, ...), kind=kOutput, calls=%fused_computation.6 | convolution fusion | flops 1074003968 | bytes 21106948 | tf_op jit(solution)/shard_map/while/body/eval_jaxpr/cond/branch_1_fun/dot_general | solution.py:58
  175.8 21.0 %reduce-scatter.3.cloned.1.call-done = f32[64,256]{1,0:T(8,128)} async-done(((f32[64,1024]{1,0:T(8,128)}), f32[64,256]{1,0:T(8,128)}) %reduce-scatter.3.cloned.1.call-update) | async-done | bytes 65552 | tf_op jit(solution)/shard_map/while/body/eval_jaxpr/reduce_scatter | solution.py:81
  203.4 5.4 all_gather.28
  209.6 35.6 %reduce-scatter.3.cloned.1.call-done = f32[64,256]{1,0:T(8,128)} async-done(((f32[64,1024]{1,0:T(8,128)}), f32[64,256]{1,0:T(8,128)}) %reduce-scatter.3.cloned.1.call-update) | async-done | bytes 65552 | tf_op jit(solution)/shard_map/while/body/eval_jaxpr/reduce_scatter | solution.py:81
  251.7 5.4 all_gather.28
  257.9 35.6 %reduce-scatter.3.cloned.1.call-done = f32[64,256]{1,0:T(8,128)} async-done(((f32[64,1024]{1,0:T(8,128)}), f32[64,256]{1,0:T(8,128)}) %reduce-scatter.3.cloned.1.call-update) | async-done | bytes 65552 | tf_op jit(solution)/shard_map/while/body/eval_jaxpr/reduce_scatter | solution.py:81
  300.0 5.4 all_gather.28
  306.2 35.6 %reduce-scatter.3.cloned.1.call-done = f32[64,256]{1,0:T(8,128)} async-done(((f32[64,1024]{1,0:T(8,128)}), f32[64,256]{1,0:T(8,128)}) %reduce-scatter.3.cloned.1.call-update) | async-done | bytes 65552 | tf_op jit(solution)/shard_map/while/body/eval_jaxpr/reduce_scatter | solution.py:81
  347.6 6.1 fusion.48
  356.2 443.4 %while.43 = (s32[]{:T(128)}, f32[64,256]{1,0:T(8,128)S(1)}, bf16[4,64,8192]{2,1,0:T(8,128)(2,1)}, bf16[4,64,1024]{2,1,0:T(8,128)(2,1)S(1)}, f32[256]{0:T(256)S(1...) while((s32[]{:T(128)}, f32[64,256]{1,0:T(8,128)S(1)}, ...), condition=%wide.region_13.14_spmd.clone, body=%wide.region_6.13_spmd.clone.sunk | while | flops 2157756928 | bytes 42672648 | solution.py:152
  356.5 5.4 all_gather.29
  362.7 44.6 %reduce-scatter.5.cloned.1.call-done = f32[64,256]{1,0:T(8,128)} async-done(((f32[64,1024]{1,0:T(8,128)}), f32[64,256]{1,0:T(8,128)}) %reduce-scatter.5.cloned.1.call-update) | async-done | bytes 65552 | tf_op jit(solution)/shard_map/while/body/eval_jaxpr/reduce_scatter | solution.py:136
  408.4 5.8 psum.23
  416.4 4.8 collective-permute-done.1
  421.2 5.4 all_gather.29
  427.5 43.4 %reduce-scatter.5.cloned.1.call-done = f32[64,256]{1,0:T(8,128)} async-done(((f32[64,1024]{1,0:T(8,128)}), f32[64,256]{1,0:T(8,128)}) %reduce-scatter.5.cloned.1.call-update) | async-done | bytes 65552 | tf_op jit(solution)/shard_map/while/body/eval_jaxpr/reduce_scatter | solution.py:136
  471.9 5.8 psum.23
  484.8 5.4 all_gather.29
  491.0 43.4 %reduce-scatter.5.cloned.1.call-done = f32[64,256]{1,0:T(8,128)} async-done(((f32[64,1024]{1,0:T(8,128)}), f32[64,256]{1,0:T(8,128)}) %reduce-scatter.5.cloned.1.call-update) | async-done | bytes 65552 | tf_op jit(solution)/shard_map/while/body/eval_jaxpr/reduce_scatter | solution.py:136
  535.4 5.8 psum.23
  548.3 5.4 all_gather.29
  553.7 23.6 %conditional.6 = (f32[64,1024]{1,0:T(8,128)S(1)}, bf16[4,64,8192]{2,1,0:T(8,128)(2,1)}, bf16[4,64,1024]{2,1,0:T(8,128)(2,1)S(1)}) conditional(s32[]{:T(128)} %convert_element_type.142, (bf16[4,64,8192]{2,1,0:T(8,128)(2,1)}, bf16[4,64,1024]{2,1,0:T(8,128)(2,1)S(1)}) %tuple.101, (bf16[64,1024]{1,0:T(8,128)(2,1)S(1)}, bf16[8192,1024]{1,0:T(8,128)(2,1)}, ...), branch_computations={%region_7.7_spmd, %region_8.8_spmd} | conditional | flops 2157445120 | bytes 39452740 | solution.py:127
  553.7 12.6 %bitcast_dynamic-update-slice_fusion.2 = (bf16[4,64,8192]{2,1,0:T(8,128)(2,1)}, bf16[64,8192]{1,0:T(8,128)(2,1)S(1)}) fusion(bf16[4,64,8192]{2,1,0:T(8,128)(2,1)} %get-tuple-element.602, s32[]{:T(128)S(6)} %select_n.88, f32[4,64,8192]{2,1,0:T(8,128)} %get-tuple-element.599, bf16[64,1024]{1,0:T(8,128)(2,1)S(1)} %get-tuple-element.597, ...), kind=kOutput, calls=%fused_computation.41 | convolution fusion | flops 1083703296 | bytes 21102596 | tf_op jit(solution)/shard_map/while/body/eval_jaxpr/cond/branch_1_fun/dot_general | solution.py:112
  566.4 11.0 %fusion.50 = f32[64,1024]{1,0:T(8,128)S(1)} fusion(bf16[64,8192]{1,0:T(8,128)(2,1)S(1)} %get-tuple-element.748, bf16[1024,8192]{1,0:T(8,128)(2,1)} %get-tuple-element.601), kind=kOutput, calls=%fused_computation.74 | convolution fusion | flops 1073741824 | bytes 18087936 | tf_op jit(solution)/shard_map/while/body/eval_jaxpr/cond/branch_1_fun/dot_general | solution.py:116
  578.1 19.8 %reduce-scatter.5.cloned.1.call-done = f32[64,256]{1,0:T(8,128)} async-done(((f32[64,1024]{1,0:T(8,128)}), f32[64,256]{1,0:T(8,128)}) %reduce-scatter.5.cloned.1.call-update) | async-done | bytes 65552 | tf_op jit(solution)/shard_map/while/body/eval_jaxpr/reduce_scatter | solution.py:136
  598.9 5.8 psum.23
  611.8 5.4 all_gather.29
  617.2 23.6 %conditional.6 = (f32[64,1024]{1,0:T(8,128)S(1)}, bf16[4,64,8192]{2,1,0:T(8,128)(2,1)}, bf16[4,64,1024]{2,1,0:T(8,128)(2,1)S(1)}) conditional(s32[]{:T(128)} %convert_element_type.142, (bf16[4,64,8192]{2,1,0:T(8,128)(2,1)}, bf16[4,64,1024]{2,1,0:T(8,128)(2,1)S(1)}) %tuple.101, (bf16[64,1024]{1,0:T(8,128)(2,1)S(1)}, bf16[8192,1024]{1,0:T(8,128)(2,1)}, ...), branch_computations={%region_7.7_spmd, %region_8.8_spmd} | conditional | flops 2157445120 | bytes 39452740 | solution.py:127
  617.2 12.6 %bitcast_dynamic-update-slice_fusion.2 = (bf16[4,64,8192]{2,1,0:T(8,128)(2,1)}, bf16[64,8192]{1,0:T(8,128)(2,1)S(1)}) fusion(bf16[4,64,8192]{2,1,0:T(8,128)(2,1)} %get-tuple-element.602, s32[]{:T(128)S(6)} %select_n.88, f32[4,64,8192]{2,1,0:T(8,128)} %get-tuple-element.599, bf16[64,1024]{1,0:T(8,128)(2,1)S(1)} %get-tuple-element.597, ...), kind=kOutput, calls=%fused_computation.41 | convolution fusion | flops 1083703296 | bytes 21102596 | tf_op jit(solution)/shard_map/while/body/eval_jaxpr/cond/branch_1_fun/dot_general | solution.py:112
  629.9 10.9 %fusion.50 = f32[64,1024]{1,0:T(8,128)S(1)} fusion(bf16[64,8192]{1,0:T(8,128)(2,1)S(1)} %get-tuple-element.748, bf16[1024,8192]{1,0:T(8,128)(2,1)} %get-tuple-element.601), kind=kOutput, calls=%fused_computation.74 | convolution fusion | flops 1073741824 | bytes 18087936 | tf_op jit(solution)/shard_map/while/body/eval_jaxpr/cond/branch_1_fun/dot_general | solution.py:116
  641.6 19.8 %reduce-scatter.5.cloned.1.call-done = f32[64,256]{1,0:T(8,128)} async-done(((f32[64,1024]{1,0:T(8,128)}), f32[64,256]{1,0:T(8,128)}) %reduce-scatter.5.cloned.1.call-update) | async-done | bytes 65552 | tf_op jit(solution)/shard_map/while/body/eval_jaxpr/reduce_scatter | solution.py:136
  662.5 5.8 psum.23
  675.4 5.4 all_gather.29
  680.8 23.6 %conditional.6 = (f32[64,1024]{1,0:T(8,128)S(1)}, bf16[4,64,8192]{2,1,0:T(8,128)(2,1)}, bf16[4,64,1024]{2,1,0:T(8,128)(2,1)S(1)}) conditional(s32[]{:T(128)} %convert_element_type.142, (bf16[4,64,8192]{2,1,0:T(8,128)(2,1)}, bf16[4,64,1024]{2,1,0:T(8,128)(2,1)S(1)}) %tuple.101, (bf16[64,1024]{1,0:T(8,128)(2,1)S(1)}, bf16[8192,1024]{1,0:T(8,128)(2,1)}, ...), branch_computations={%region_7.7_spmd, %region_8.8_spmd} | conditional | flops 2157445120 | bytes 39452740 | solution.py:127
  680.8 12.6 %bitcast_dynamic-update-slice_fusion.2 = (bf16[4,64,8192]{2,1,0:T(8,128)(2,1)}, bf16[64,8192]{1,0:T(8,128)(2,1)S(1)}) fusion(bf16[4,64,8192]{2,1,0:T(8,128)(2,1)} %get-tuple-element.602, s32[]{:T(128)S(6)} %select_n.88, f32[4,64,8192]{2,1,0:T(8,128)} %get-tuple-element.599, bf16[64,1024]{1,0:T(8,128)(2,1)S(1)} %get-tuple-element.597, ...), kind=kOutput, calls=%fused_computation.41 | convolution fusion | flops 1083703296 | bytes 21102596 | tf_op jit(solution)/shard_map/while/body/eval_jaxpr/cond/branch_1_fun/dot_general | solution.py:112
  693.4 11.0 %fusion.50 = f32[64,1024]{1,0:T(8,128)S(1)} fusion(bf16[64,8192]{1,0:T(8,128)(2,1)S(1)} %get-tuple-element.748, bf16[1024,8192]{1,0:T(8,128)(2,1)} %get-tuple-element.601), kind=kOutput, calls=%fused_computation.74 | convolution fusion | flops 1073741824 | bytes 18087936 | tf_op jit(solution)/shard_map/while/body/eval_jaxpr/cond/branch_1_fun/dot_general | solution.py:116
  705.2 18.9 %reduce-scatter.5.cloned.1.call-done = f32[64,256]{1,0:T(8,128)} async-done(((f32[64,1024]{1,0:T(8,128)}), f32[64,256]{1,0:T(8,128)}) %reduce-scatter.5.cloned.1.call-update) | async-done | bytes 65552 | tf_op jit(solution)/shard_map/while/body/eval_jaxpr/reduce_scatter | solution.py:136
  725.1 5.8 psum.23
  738.0 5.4 all_gather.29
  743.4 23.6 %conditional.6 = (f32[64,1024]{1,0:T(8,128)S(1)}, bf16[4,64,8192]{2,1,0:T(8,128)(2,1)}, bf16[4,64,1024]{2,1,0:T(8,128)(2,1)S(1)}) conditional(s32[]{:T(128)} %convert_element_type.142, (bf16[4,64,8192]{2,1,0:T(8,128)(2,1)}, bf16[4,64,1024]{2,1,0:T(8,128)(2,1)S(1)}) %tuple.101, (bf16[64,1024]{1,0:T(8,128)(2,1)S(1)}, bf16[8192,1024]{1,0:T(8,128)(2,1)}, ...), branch_computations={%region_7.7_spmd, %region_8.8_spmd} | conditional | flops 2157445120 | bytes 39452740 | solution.py:127
  743.4 12.6 %bitcast_dynamic-update-slice_fusion.2 = (bf16[4,64,8192]{2,1,0:T(8,128)(2,1)}, bf16[64,8192]{1,0:T(8,128)(2,1)S(1)}) fusion(bf16[4,64,8192]{2,1,0:T(8,128)(2,1)} %get-tuple-element.602, s32[]{:T(128)S(6)} %select_n.88, f32[4,64,8192]{2,1,0:T(8,128)} %get-tuple-element.599, bf16[64,1024]{1,0:T(8,128)(2,1)S(1)} %get-tuple-element.597, ...), kind=kOutput, calls=%fused_computation.41 | convolution fusion | flops 1083703296 | bytes 21102596 | tf_op jit(solution)/shard_map/while/body/eval_jaxpr/cond/branch_1_fun/dot_general | solution.py:112
  756.0 11.0 %fusion.50 = f32[64,1024]{1,0:T(8,128)S(1)} fusion(bf16[64,8192]{1,0:T(8,128)(2,1)S(1)} %get-tuple-element.748, bf16[1024,8192]{1,0:T(8,128)(2,1)} %get-tuple-element.601), kind=kOutput, calls=%fused_computation.74 | convolution fusion | flops 1073741824 | bytes 18087936 | tf_op jit(solution)/shard_map/while/body/eval_jaxpr/cond/branch_1_fun/dot_general | solution.py:116
  767.8 18.0 %reduce-scatter.5.cloned.1.call-done = f32[64,256]{1,0:T(8,128)} async-done(((f32[64,1024]{1,0:T(8,128)}), f32[64,256]{1,0:T(8,128)}) %reduce-scatter.5.cloned.1.call-update) | async-done | bytes 65552 | tf_op jit(solution)/shard_map/while/body/eval_jaxpr/reduce_scatter | solution.py:136
  786.8 5.8 psum.23
  808.0 21.2 %psum.20 = f32[1,256]{1,0:T(1,128)} all-reduce(f32[1,256]{1,0:T(1,128)S(1)} %bitcast.82), channel_id=1, replica_groups=mesh['dp'=2,'pipe'=4,'mp'=4] {'dp'}, use_global_device_ids=true, to_apply=%region_14.15 | all-reduce | flops 256 | bytes 2048 | tf_op jit(solution)/shard_map/psum | solution.py:182
  829.4 81.4 %all-gather.5.cloned.1.call-done = bf16[512,8192]{1,0:T(8,128)(2,1)} async-done(((bf16[256,8192]{1,0:T(8,128)(2,1)}), bf16[512,8192]{1,0:T(8,128)(2,1)}) %all-gather.5.cloned.1.call-update) | async-done | bytes 8388624 | tf_op jit(solution)/shard_map/all_gather | solution.py:168
  910.8 10.5 %fusion.43 = bf16[1,8192,512]{2,1,0:T(8,128)(2,1)} fusion(bf16[512,8192]{1,0:T(8,128)(2,1)} %all-gather.5.cloned.1.call-done, bf16[512,512]{1,0:T(8,128)(2,1)S(1)} %bitcast.80), kind=kOutput, calls=%fused_computation.63 | convolution fusion | flops 4299161600 | bytes 17301504 | tf_op jit(solution)/shard_map/dot_general | solution.py:174
  921.3 93.5 %all-gather.3.cloned.1.call-done = bf16[512,8192]{1,0:T(8,128)(2,1)} async-done(((bf16[256,8192]{1,0:T(8,128)(2,1)}), bf16[512,8192]{1,0:T(8,128)(2,1)}) %all-gather.3.cloned.1.call-update) | async-done | bytes 8388624 | tf_op jit(solution)/shard_map/all_gather | solution.py:167
  1014.8 10.2 fusion.42
  (209 shorter events, 141.4 us)
Async XLA Ops:
  8.7 4.5 copy-start.3
  13.2 41.4 %reduce-scatter.3.cloned.1.call-start = ((), (), s32[]{:S(2)}) async-start(), calls=%async_computation.5 | async-start | bytes 327680 | tf_op jit(solution)/shard_map/while/body/eval_jaxpr/reduce_scatter | solution.py:81
  20.7 11.3 %copy-start = (bf16[8192,1024]{1,0:T(8,128)(2,1)S(1)}, bf16[8192,1024]{1,0:T(8,128)(2,1)}, u32[]{:S(2)}) copy-start(bf16[8192,1024]{1,0:T(8,128)(2,1)} %get-tuple-element.574) | copy-start | bytes 50331652 | tf_op jit(solution)/shard_map/while/body/eval_jaxpr/cond
  35.1 0.7 copy-start.1
  55.5 5.0 collective-permute-start
  60.4 40.7 %reduce-scatter.3.cloned.1.call-start = ((), (), s32[]{:S(2)}) async-start(), calls=%async_computation.5 | async-start | bytes 327680 | tf_op jit(solution)/shard_map/while/body/eval_jaxpr/reduce_scatter | solution.py:81
  66.7 11.3 %copy-start = (bf16[8192,1024]{1,0:T(8,128)(2,1)S(1)}, bf16[8192,1024]{1,0:T(8,128)(2,1)}, u32[]{:S(2)}) copy-start(bf16[8192,1024]{1,0:T(8,128)(2,1)} %get-tuple-element.574) | copy-start | bytes 50331652 | tf_op jit(solution)/shard_map/while/body/eval_jaxpr/cond
  81.1 0.7 copy-start.1
  102.0 5.0 collective-permute-start
  106.9 41.6 %reduce-scatter.3.cloned.1.call-start = ((), (), s32[]{:S(2)}) async-start(), calls=%async_computation.5 | async-start | bytes 327680 | tf_op jit(solution)/shard_map/while/body/eval_jaxpr/reduce_scatter | solution.py:81
  113.2 11.3 %copy-start = (bf16[8192,1024]{1,0:T(8,128)(2,1)S(1)}, bf16[8192,1024]{1,0:T(8,128)(2,1)}, u32[]{:S(2)}) copy-start(bf16[8192,1024]{1,0:T(8,128)(2,1)} %get-tuple-element.574) | copy-start | bytes 50331652 | tf_op jit(solution)/shard_map/while/body/eval_jaxpr/cond
  127.6 0.7 copy-start.1
  149.3 5.0 collective-permute-start
  154.3 42.5 %reduce-scatter.3.cloned.1.call-start = ((), (), s32[]{:S(2)}) async-start(), calls=%async_computation.5 | async-start | bytes 327680 | tf_op jit(solution)/shard_map/while/body/eval_jaxpr/reduce_scatter | solution.py:81
  160.6 11.3 %copy-start = (bf16[8192,1024]{1,0:T(8,128)(2,1)S(1)}, bf16[8192,1024]{1,0:T(8,128)(2,1)}, u32[]{:S(2)}) copy-start(bf16[8192,1024]{1,0:T(8,128)(2,1)} %get-tuple-element.574) | copy-start | bytes 50331652 | tf_op jit(solution)/shard_map/while/body/eval_jaxpr/cond
  175.0 0.7 copy-start.1
  197.7 5.0 collective-permute-start
  202.6 42.5 %reduce-scatter.3.cloned.1.call-start = ((), (), s32[]{:S(2)}) async-start(), calls=%async_computation.5 | async-start | bytes 327680 | tf_op jit(solution)/shard_map/while/body/eval_jaxpr/reduce_scatter | solution.py:81
  208.9 0.7 copy-start.1
  246.0 5.0 collective-permute-start
  251.0 42.5 %reduce-scatter.3.cloned.1.call-start = ((), (), s32[]{:S(2)}) async-start(), calls=%async_computation.5 | async-start | bytes 327680 | tf_op jit(solution)/shard_map/while/body/eval_jaxpr/reduce_scatter | solution.py:81
  257.2 0.7 copy-start.1
  294.3 5.0 collective-permute-start
  299.3 42.5 %reduce-scatter.3.cloned.1.call-start = ((), (), s32[]{:S(2)}) async-start(), calls=%async_computation.5 | async-start | bytes 327680 | tf_op jit(solution)/shard_map/while/body/eval_jaxpr/reduce_scatter | solution.py:81
  305.5 0.7 copy-start.1
  342.6 5.0 collective-permute-start
  353.7 2.6 copy-start.4
  356.4 50.9 %reduce-scatter.5.cloned.1.call-start = ((), (), s32[]{:S(2)}) async-start(), calls=%async_computation.6 | async-start | bytes 327680 | tf_op jit(solution)/shard_map/while/body/eval_jaxpr/reduce_scatter | solution.py:136
  362.0 0.7 copy-start.2
  415.1 6.2 collective-permute-start.1
  421.2 49.7 %reduce-scatter.5.cloned.1.call-start = ((), (), s32[]{:S(2)}) async-start(), calls=%async_computation.6 | async-start | bytes 327680 | tf_op jit(solution)/shard_map/while/body/eval_jaxpr/reduce_scatter | solution.py:136
  426.7 0.7 copy-start.2
  478.6 6.2 collective-permute-start.1
  484.8 49.6 %reduce-scatter.5.cloned.1.call-start = ((), (), s32[]{:S(2)}) async-start(), calls=%async_computation.6 | async-start | bytes 327680 | tf_op jit(solution)/shard_map/while/body/eval_jaxpr/reduce_scatter | solution.py:136
  490.2 0.7 copy-start.2
  542.1 6.2 collective-permute-start.1
  548.3 49.6 %reduce-scatter.5.cloned.1.call-start = ((), (), s32[]{:S(2)}) async-start(), calls=%async_computation.6 | async-start | bytes 327680 | tf_op jit(solution)/shard_map/while/body/eval_jaxpr/reduce_scatter | solution.py:136
  577.3 0.7 copy-start.2
  605.6 6.2 collective-permute-start.1
  611.8 49.7 %reduce-scatter.5.cloned.1.call-start = ((), (), s32[]{:S(2)}) async-start(), calls=%async_computation.6 | async-start | bytes 327680 | tf_op jit(solution)/shard_map/while/body/eval_jaxpr/reduce_scatter | solution.py:136
  640.9 0.7 copy-start.2
  669.2 6.2 collective-permute-start.1
  675.4 48.7 %reduce-scatter.5.cloned.1.call-start = ((), (), s32[]{:S(2)}) async-start(), calls=%async_computation.6 | async-start | bytes 327680 | tf_op jit(solution)/shard_map/while/body/eval_jaxpr/reduce_scatter | solution.py:136
  704.4 0.7 copy-start.2
  731.8 6.2 collective-permute-start.1
  738.0 47.8 %reduce-scatter.5.cloned.1.call-start = ((), (), s32[]{:S(2)}) async-start(), calls=%async_computation.6 | async-start | bytes 327680 | tf_op jit(solution)/shard_map/while/body/eval_jaxpr/reduce_scatter | solution.py:136
  767.0 0.7 copy-start.2
  793.5 6.2 collective-permute-start.1
  799.6 111.1 %all-gather.5.cloned.1.call-start = ((), (), s32[]{:S(2)}) async-start(), calls=%async_computation.4 | async-start | bytes 12582912 | tf_op jit(solution)/shard_map/all_gather | solution.py:168
  800.2 214.6 %all-gather.3.cloned.1.call-start = ((), (), s32[]{:S(2)}) async-start(), calls=%async_computation.3 | async-start | bytes 12582912 | tf_op jit(solution)/shard_map/all_gather | solution.py:167
  804.4 24.9 %all-to-all-start = ((bf16[2,256,2,512]{3,1,0,2:T(8,128)(2,1)}), bf16[2,256,2,512]{3,1,0,2:T(8,128)(2,1)S(1)}, u32[]{:S(2)}, u32[]{:S(2)}) async-start(bf16[2,256,2,512]{3,1,0,2:T(8,128)(2,1)} %copy.10), calls=%async_computation.2 | async-start | bytes 2097152 | tf_op jit(solution)/shard_map/all_to_all | solution.py:165
Sparse Core Ops, SparseCore 0:
  35.9 18.6 reduce-scatter.2
  82.0 19.0 reduce-scatter.2
  128.5 19.9 reduce-scatter.2
  175.9 20.8 reduce-scatter.2
  209.7 35.3 reduce-scatter.2
  258.0 35.3 reduce-scatter.2
  306.3 35.3 reduce-scatter.2
  362.8 44.4 reduce-scatter.4
  427.5 43.2 reduce-scatter.4
  491.1 43.2 reduce-scatter.4
  578.2 19.6 reduce-scatter.4
  641.7 19.7 reduce-scatter.4
  705.2 18.7 reduce-scatter.4
  767.9 17.8 reduce-scatter.4
Sparse Core Ops, SparseCore 1:
  801.6 109.1 all-gather.4
  912.8 102.0 all-gather.2
where the time goes:
time: 1030 us
  waiting for transfers between devices  615 us (60%)
  matrix products  169 us (16%)
  blocking collectives  138 us (13%)
  starting transfers between devices  36.5 us (4%)
  other arithmetic  33.5 us (3%)
  local copies, waits for them, and re-layouts  23.8 us (2%)
  between operations  15.3 us (1%)
    reduce_scatter x7, waiting for transfers between devices, backward_turn(): lax.psum_scatter(norm_part, 'mp', scatter_dimension=1, tiled=True)  208 us
    reduce_scatter x7, waiting for transfers between devices, forward_turn(): branch_sum = lax.psum_scatter(branch, 'mp', scatter_dimension=1, tiled=True)  186 us
    all_gather x1, waiting for transfers between devices, shards(): pregrad_piece = lax.all_gather(pregrad_all, 'dp', axis=0, tiled=True)  93.5 us
    all_gather x1, waiting for transfers between devices, shards(): activated_piece = lax.all_gather(activated_all, 'dp', axis=0, tiled=True)  81.4 us
    dot_general x4, matrix products, backward_active(): lax.dot_general(gathered, weight_second, CONTRACT_LAST, preferred_element...  50.5 us
    ppermute x14, waiting for transfers between devices, shifted(): return lax.ppermute(shard, axis, pairs)  44.9 us
    dot_general x4, matrix products, backward_active(): lax.dot_general(pre_grad, weight_first, CONTRACT_LAST, preferred_element_...  43.8 us
    dot_general x4, matrix products, forward_active(): jnp.dot(normed, weight_first, preferred_element_type=jnp.float32)  41.4 us
  transfers between devices with their start and end apart: 31, of which 30 were waited for; matrix products, arithmetic and copies ran while one was open for 1% of the time, Pallas kernels for 0%

commit v1 on v0

v1 whole, which is shorter than its diff:
```python
import functools
import math

import jax
import jax.numpy as jnp
from jax import lax
from jax.experimental import pallas as pl
from jax.experimental.pallas import tpu as pltpu
from jax.sharding import PartitionSpec as P

GELU_COEF = math.sqrt(2.0 / math.pi)
CUBIC_COEF = 0.044715
NORM_EPS = 1e-06
CONTRACT_LAST = (((1,), (1,)), ((), ()))
CONTRACT_FIRST = (((0,), (0,)), ((), ()))
MESH = pl.DeviceIdType.MESH


def gelu_parts(values):
    square = values * values
    half = 0.5 + 0.5 * jnp.tanh(values * (GELU_COEF + GELU_COEF * CUBIC_COEF * square))
    bend = values * (half - half * half)
    derivative = half + bend * (2.0 * GELU_COEF + 6.0 * GELU_COEF * CUBIC_COEF * square)
    return (values * half, derivative)


def inverse_rms(values):
    return lax.rsqrt(jnp.mean(values * values, axis=1, keepdims=True) + NORM_EPS)


def relay(
    sizes,
    x_ref,
    cot_ref,
    gain_ref,
    w1_hbm,
    w2_hbm,
    z_out,
    p_out,
    u_out,
    e_out,
    gain_out,
    w1,
    w2,
    z_keep,
    p_keep,
    h_all,
    u_all,
    e_all,
    acc,
    f_send,
    f_recv,
    b_send,
    b_recv,
    h_hop,
    g_hop,
    gain_part,
    gain_recv,
    w1_sem,
    w2_sem,
    z_sem,
    p_sem,
    out_sem,
    x_ssem,
    x_rsem,
    hop_sem,
    ag_ssem,
    ag_rsem,
    dp_ssem,
    dp_rsem,
    rs_ssem,
    rs_rsem,
    gain_ssem,
    gain_rsem,
):
    stages, parts, replicas = sizes
    sec = lax.axis_index("pipe")
    me = lax.axis_index("mp")
    rep = lax.axis_index("dp")
    tiles, full, tile = w1.shape
    rows = h_all.shape[0]
    own = rows // parts
    width = full // parts
    first = sec == 0
    last = sec == stages - 1

    def w_copies(i):
        start = pl.multiple_of(i * tile, tile)
        return (
            pltpu.make_async_copy(w1_hbm.at[:, pl.ds(start, tile)], w1.at[i], w1_sem.at[i]),
            pltpu.make_async_copy(w2_hbm.at[pl.ds(start, tile), :], w2.at[i], w2_sem.at[i]),
        )

    for i in range(tiles):
        for copy in w_copies(i):
            copy.start()

    barrier = pltpu.get_barrier_semaphore()
    peers = []
    for d in range(replicas):
        for j in range(parts):
            if d or j:
                peers.append((d, j, lax.rem(rep + d, replicas), lax.rem(me + j, parts)))
    for _, _, other, part in peers:
        pl.semaphore_signal(
            barrier, inc=1, device_id={"dp": other, "mp": part}, device_id_type=MESH
        )
    for step in (1, stages - 1):
        pl.semaphore_signal(
            barrier,
            inc=1,
            device_id={"pipe": lax.rem(sec + step, stages)},
            device_id_type=MESH,
        )
    pl.semaphore_wait(barrier, len(peers) + 2)

    my_rows = pl.ds(pl.multiple_of(me * own, own), own)
    my_cols = pl.ds(pl.multiple_of(me * width, width), width)

    def remote(src, dst, ssem, rsem, where):
        return pltpu.make_async_remote_copy(
            src_ref=src,
            dst_ref=dst,
            send_sem=ssem,
            recv_sem=rsem,
            device_id=where,
            device_id_type=MESH,
        )

    def others():
        return [(j, lax.rem(me + j, parts)) for j in range(1, parts)]

    def feature_copies(src, dst):
        return [
            remote(src, dst.at[:, my_cols], x_ssem.at[j], x_rsem.at[j], {"mp": part})
            for j, part in others()
        ]

    def row_copies(dst, which):
        return [
            remote(
                dst.at[my_rows, :],
                dst.at[my_rows, :],
                ag_ssem.at[which, j],
                ag_rsem.at[which, j],
                {"mp": part},
            )
            for j, part in others()
        ]

    def sum_copies(src, dst, which):
        return [
            remote(
                src.at[pl.ds(pl.multiple_of(part * own, own), own), :],
                dst.at[j],
                rs_ssem.at[which, j],
                rs_rsem.at[which, j],
                {"mp": part},
            )
            for j, part in others()
        ]

    def replica_copies(ref, which):
        return [
            remote(
                ref.at[0],
                ref.at[d],
                dp_ssem.at[which, d],
                dp_rsem.at[which, d],
                {"dp": lax.rem(rep + d, replicas)},
            )
            for d in range(1, replicas)
        ]

    def start(copies):
        for copy in copies:
            copy.start()

    def finish(copies):
        for copy in copies:
            copy.wait()

    def forward_hop():
        return remote(
            h_hop,
            h_all.at[my_rows, :],
            hop_sem.at[0],
            hop_sem.at[1],
            {"pipe": lax.rem(sec + 1, stages)},
        )

    def backward_hop():
        return remote(
            g_hop,
            e_all.at[0, my_rows, :],
            hop_sem.at[2],
            hop_sem.at[3],
            {"pipe": lax.rem(sec + stages - 1, stages)},
        )

    @pl.when(last)
    def _():
        copies = feature_copies(cot_ref, e_all.at[0])
        start(copies)
        e_all[0, :, my_cols] = cot_ref[...]
        finish(copies)
        start(replica_copies(e_all, 1))

    @pl.when(first)
    def _():
        copies = feature_copies(x_ref, h_all)
        start(copies)
        h_all[:, my_cols] = x_ref[...]
        finish(copies)

    @pl.when(jnp.logical_not(first))
    def _():
        forward_hop().wait_recv()
        copies = row_copies(h_all, 0)
        start(copies)
        finish(copies)

    values = h_all[...].astype(jnp.float32)
    u_all[0] = (values * inverse_rms(values) * gain_ref[...]).astype(jnp.bfloat16)
    start(replica_copies(u_all, 0))
    acc[...] = jnp.zeros_like(acc)

    def z_copy(d, i):
        return pltpu.make_async_copy(
            z_keep.at[d, i],
            z_out.at[pl.ds(d * rows, rows), pl.ds(pl.multiple_of(i * tile, tile), tile)],
            z_sem.at[d, i],
        )

    def p_copy(d, i):
        return pltpu.make_async_copy(
            p_keep.at[d, i],
            p_out.at[pl.ds(d * rows, rows), pl.ds(pl.multiple_of(i * tile, tile), tile)],
            p_sem.at[d, i],
        )

    def activate(d, i):
        gate = jnp.dot(u_all[d], w1[i], preferred_element_type=jnp.float32)
        output, slope = gelu_parts(gate)
        output = output.astype(jnp.bfloat16)
        z_keep[d, i] = output
        p_keep[d, i] = slope.astype(jnp.bfloat16)
        return output

    def pregrad(d, i):
        inner = lax.dot_general(
            e_all[d], w2[i], CONTRACT_LAST, preferred_element_type=jnp.float32
        )
        grad = (inner * p_keep[d, i].astype(jnp.float32)).astype(jnp.bfloat16)
        p_keep[d, i] = grad
        return grad

    @pl.loop(0, tiles)
    def _(i):
        for copy in w_copies(i):
            copy.wait()
        output = activate(0, i)

        @pl.when(jnp.logical_not(last))
        def _():
            acc[...] += jnp.dot(output, w2[i], preferred_element_type=jnp.float32)

    @pl.when(jnp.logical_not(last))
    def _():
        f_send[...] = acc[...].astype(jnp.bfloat16)
        copies = sum_copies(f_send, f_recv, 0)
        start(copies)
        total = h_all[my_rows, :].astype(jnp.float32) + acc[my_rows, :]
        for j, copy in enumerate(copies):
            copy.wait()
            total += f_recv[j + 1].astype(jnp.float32)
        h_hop[...] = total.astype(jnp.bfloat16)
        forward_hop().start()

    @pl.loop(0, tiles)
    def _(i):
        z_copy(0, i).start()

    def replica_forward():
        finish(replica_copies(u_all, 0))
        for d in range(1, replicas):

            @pl.loop(0, tiles)
            def _(i):
                activate(d, i)
                z_copy(d, i).start()

    @pl.when(jnp.logical_not(last))
    def _():
        replica_forward()
        forward_hop().wait_send()
        backward_hop().wait_recv()
        copies = row_copies(e_all.at[0], 1)
        start(copies)
        finish(copies)
        start(replica_copies(e_all, 1))

    acc[...] = jnp.zeros_like(acc)

    @pl.loop(0, tiles)
    def _(i):
        grad = pregrad(0, i)
        acc[...] += lax.dot_general(
            grad, w1[i], CONTRACT_LAST, preferred_element_type=jnp.float32
        )
        p_copy(0, i).start()

    @pl.when(jnp.logical_not(first))
    def _():
        b_send[...] = acc[...].astype(jnp.bfloat16)
        copies = sum_copies(b_send, b_recv, 1)
        start(copies)
        mine = h_all[my_rows, :].astype(jnp.float32)
        scale = inverse_rms(mine)
        unit = mine * scale
        total = acc[my_rows, :]
        for j, copy in enumerate(copies):
            copy.wait()
            total += b_recv[j + 1].astype(jnp.float32)
        scaled = total * gain_ref[...]
        row_dot = jnp.sum(scaled * unit, axis=1, keepdims=True)
        previous = e_all[0, my_rows, :].astype(jnp.float32) + scale * (
            scaled - unit * (row_dot / full)
        )
        g_hop[...] = previous.astype(jnp.bfloat16)
        backward_hop().start()

    values = h_all[...].astype(jnp.float32)
    terms = acc[...] * (values * inverse_rms(values))
    gain_part[...] = jnp.sum(terms.reshape(rows // 8, 8, full), axis=0)
    gain_copies = [
        remote(
            gain_part.at[:, pl.ds(pl.multiple_of(part * width, width), width)],
            gain_recv.at[d * parts + j],
            gain_ssem.at[d * parts + j],
            gain_rsem.at[d * parts + j],
            {"dp": other, "mp": part},
        )
        for d, j, other, part in peers
    ]
    start(gain_copies)

    @pl.when(last)
    def _():
        replica_forward()

    finish(replica_copies(e_all, 1))
    for d in range(1, replicas):

        @pl.loop(0, tiles)
        def _(i):
            pregrad(d, i)
            p_copy(d, i).start()

    outs = []
    for d in range(replicas):
        place = pl.ds(d * rows, rows)
        outs.append(pltpu.make_async_copy(u_all.at[d], u_out.at[place, :], out_sem.at[0, d]))
        outs.append(pltpu.make_async_copy(e_all.at[d], e_out.at[place, :], out_sem.at[1, d]))
    start(outs)
    total = gain_part[:, my_cols]
    for (d, j, _, _), copy in zip(peers, gain_copies):
        copy.wait()
        total += gain_recv[d * parts + j]
    gain_out[...] = jnp.sum(total, axis=0, keepdims=True)

    for d in range(replicas):

        @pl.loop(0, tiles)
        def _(i):
            z_copy(d, i).wait()
            p_copy(d, i).wait()

    finish(outs)

    @pl.when(jnp.logical_not(first))
    def _():
        backward_hop().wait_send()


def shards(inputs, cotangent, gain, weight_in, weight_out):
    stages = lax.axis_size("pipe")
    parts = lax.axis_size("mp")
    replicas = lax.axis_size("dp")
    micro, row_count, width = inputs.shape
    rows = micro * row_count
    full = gain.shape[1]
    hidden = weight_in.shape[2]
    tile = math.gcd(hidden, 1024)
    tiles = hidden // tile
    own = rows // parts
    half = full // replicas
    bf16, f32 = jnp.bfloat16, jnp.float32
    vmem = pl.BlockSpec(memory_space=pltpu.VMEM)
    anywhere = pl.BlockSpec(memory_space=pl.ANY)
    dma = pltpu.SemaphoreType.DMA
    z_all, p_all, u_all, e_all, gain_total = pl.pallas_call(
        functools.partial(relay, (stages, parts, replicas)),
        name="relay",
        out_shape=(
            jax.ShapeDtypeStruct((replicas * rows, hidden), bf16),
            jax.ShapeDtypeStruct((replicas * rows, hidden), bf16),
            jax.ShapeDtypeStruct((replicas * rows, full), bf16),
            jax.ShapeDtypeStruct((replicas * rows, full), bf16),
            jax.ShapeDtypeStruct((1, width), f32),
        ),
        in_specs=[vmem, vmem, vmem, anywhere, anywhere],
        out_specs=(anywhere, anywhere, anywhere, anywhere, vmem),
        scratch_shapes=[
            pltpu.VMEM((tiles, full, tile), bf16),
            pltpu.VMEM((tiles, tile, full), bf16),
            pltpu.VMEM((replicas, tiles, rows, tile), bf16),
            pltpu.VMEM((replicas, tiles, rows, tile), bf16),
            pltpu.VMEM((rows, full), bf16),
            pltpu.VMEM((replicas, rows, full), bf16),
            pltpu.VMEM((replicas, rows, full), bf16),
            pltpu.VMEM((rows, full), f32),
            pltpu.VMEM((rows, full), bf16),
            pltpu.VMEM((parts, own, full), bf16),
            pltpu.VMEM((rows, full), bf16),
            pltpu.VMEM((parts, own, full), bf16),
            pltpu.VMEM((own, full), bf16),
            pltpu.VMEM((own, full), bf16),
            pltpu.VMEM((8, full), f32),
            pltpu.VMEM((replicas * parts, 8, width), f32),
            dma((tiles,)),
            dma((tiles,)),
            dma((replicas, tiles)),
            dma((replicas, tiles)),
            dma((2, replicas)),
            dma((parts,)),
            dma((parts,)),
            dma((4,)),
            dma((2, parts)),
            dma((2, parts)),
            dma((2, replicas)),
            dma((2, replicas)),
            dma((2, parts)),
            dma((2, parts)),
            dma((replicas * parts,)),
            dma((replicas * parts,)),
        ],
        compiler_params=pltpu.CompilerParams(
            collective_id=0, has_side_effects=True, vmem_limit_bytes=67043328
        ),
    )(
        inputs.reshape(rows, width),
        cotangent.reshape(rows, width),
        gain,
        weight_in[0],
        weight_out[0],
    )
    begin = lax.axis_index("dp") * half
    u_cols = lax.dynamic_slice_in_dim(u_all, begin, half, 1)
    e_cols = lax.dynamic_slice_in_dim(e_all, begin, half, 1)
    grad_first = lax.dot_general(u_cols, p_all, CONTRACT_FIRST, preferred_element_type=f32)
    grad_second = lax.dot_general(z_all, e_cols, CONTRACT_FIRST, preferred_element_type=f32)
    return (grad_first.astype(bf16)[None], grad_second.astype(bf16)[None], gain_total)


def solution(mesh):
    in_specs = (
        P(None, "dp", "mp"),
        P(None, "dp", "mp"),
        P("pipe", None),
        P("pipe", None, "mp"),
        P("pipe", "mp", None),
    )
    out_specs = (P("pipe", "dp", "mp"), P("pipe", "mp", "dp"), P("pipe", "mp"))
    return jax.shard_map(shards, mesh=mesh, in_specs=in_specs, out_specs=out_specs, check_vma=False)
```

time: 1030 us -> 248 us (0.24)
  waiting for transfers between devices: 615 us -> 0 us
  Pallas kernels: 0 us -> 226 us
  matrix products: 169 us -> 18.6 us
  blocking collectives: 138 us -> 0 us
  starting transfers between devices: 36.5 us -> 0 us
  other arithmetic: 33.5 us -> 0 us
  local copies, waits for them, and re-layouts: 23.8 us -> 0.57 us
  between operations: 15.3 us -> 0.67 us
    reduce_scatter x14 -> x0, waiting for transfers between devices: 394 us -> none  [the longest x7 208 us: backward_turn(): lax.psum_scatter(norm_part, 'mp', scatter_dimension=1, tiled=True)]
    pallas_call x0 -> x1, Pallas kernels: none -> 226 us  [shards(): pl.pallas_call(functools.partial(relay, (stages, parts, replicas)), name=...]
    all_gather x2 -> x0, waiting for transfers between devices: 175 us -> none  [the longest x1 93.5 us: shards(): pregrad_piece = lax.all_gather(pregrad_all, 'dp', axis=0, tiled=True)]
    dot_general x18 -> x2, matrix products: 169 us -> 18.6 us  [the longest x1 11.7 us: shards(): lax.dot_general(u_cols, p_all, CONTRACT_FIRST, preferred_element_type=f32)]
    all_gather x14 -> x0, blocking collectives: 76.9 us -> none  [the longest x7 38.9 us: forward_turn(): whole_rows = lax.all_gather(segment_input, 'mp', axis=1, tiled=True)]
    psum x8 -> x0, blocking collectives: 61.5 us -> none  [the longest x7 40.3 us: backward_turn(): row_dot = lax.psum(jnp.sum(scaled * unit_own, axis=1), 'mp')]
    ppermute x14 -> x0, waiting for transfers between devices: 44.9 us -> none  [shifted(): return lax.ppermute(shard, axis, pairs)]
    ppermute x14 -> x0, starting transfers between devices: 32.7 us -> none  [shifted(): return lax.ppermute(shard, axis, pairs)]
  transfers between devices with their start and end apart: 31 -> 0, of which waited for: 30 -> 0; matrix products, arithmetic and copies ran while one was open for 1% -> 0% of each run, Pallas kernels for 0% -> 0%
where the time goes in v1:
time: 248 us; the launch traced here: 246 us
  Pallas kernels  226 us (91%)
  matrix products  18.6 us (8%)
    pallas_call x1, Pallas kernels, shards(): pl.pallas_call(functools.partial(relay, (stages, parts, replicas)), name=...  226 us
    dot_general x1, matrix products, shards(): lax.dot_general(u_cols, p_all, CONTRACT_FIRST, preferred_element_type=f32)  11.7 us
    dot_general x1, matrix products, shards(): lax.dot_general(z_all, e_cols, CONTRACT_FIRST, preferred_element_type=f32)  6.98 us

profile of v1, /device:TPU:0, one launch (start us, length us, event | category | flops | bytes accessed | tf_op | source)
XLA Modules:
  0.0 246.2 jit_solution(9317028539099834611)
XLA Ops:
  0.6 226.3 %relay.1 = (bf16[512,8192]{1,0:T(8,128)(2,1)}, bf16[512,8192]{1,0:T(8,128)(2,1)}, bf16[512,1024]{1,0:T(8,128)(2,1)}, bf16[512,1024]{1,0:T(8,128)(2,1)}, f32[1,256]{1,0:T(1,128)}) custom-call(bf16[256,256]{1,0:T(8,128)(2,1)} %bitcast.12, bf16[256,256]{1,0:T(8,128)(2,1)} %bitcast.13, f32[1,1024]{1,0:T(1,128)} %gain_ref.1, bf16[1024,8192]{1,0:T(8,128)(2,1)} %bitcast.10, ...), custom_call_target="tpu_custom_call" | custom-call | tf_op jit(solution)/shard_map/relay/pallas_call | solution.py:402
  227.0 0.0 copy-start.1
  227.0 0.0 copy-start.2
  227.0 11.7 %fusion = bf16[1,512,8192]{2,1,0:T(8,128)(2,1)} fusion(bf16[512,8192]{1,0:T(8,128)(2,1)} %get-tuple-element.9, bf16[512,1024]{1,0:T(8,128)(2,1)} %get-tuple-element.8, s32[]{:T(128)S(6)} %select_n.4), kind=kOutput, calls=%fused_computation.2 | convolution fusion | flops 4299161600 | bytes 17301508 | tf_op jit(solution)/shard_map/dot_general | solution.py:461
  238.6 0.0 copy-done.1
  238.6 0.0 copy-done.2
  238.6 0.0 copy-start
  238.6 7.0 %fusion.1 = bf16[1,8192,512]{2,1,0:T(8,128)(2,1)} fusion(bf16[512,8192]{1,0:T(8,128)(2,1)S(1)} %copy-done.1, bf16[512,1024]{1,0:T(8,128)(2,1)S(1)} %copy-done.2, s32[]{:T(128)S(6)} %select_n.4), kind=kOutput, calls=%fused_computation.3 | convolution fusion | flops 4299161600 | bytes 17301508 | tf_op jit(solution)/shard_map/dot_general | solution.py:462
  245.6 0.0 copy-done
  245.6 0.6 copy.9
Async XLA Ops:
  227.0 11.7 %copy-start.1 = (bf16[512,8192]{1,0:T(8,128)(2,1)S(1)}, bf16[512,8192]{1,0:T(8,128)(2,1)}, u32[]{:S(2)}) copy-start(bf16[512,8192]{1,0:T(8,128)(2,1)} %get-tuple-element.10) | copy-start | bytes 25165828
  227.0 11.7 %copy-start.2 = (bf16[512,1024]{1,0:T(8,128)(2,1)S(1)}, bf16[512,1024]{1,0:T(8,128)(2,1)}, u32[]{:S(2)}) copy-start(bf16[512,1024]{1,0:T(8,128)(2,1)} %get-tuple-element.11) | copy-start | bytes 3145732
  238.6 7.0 %copy-start = (f32[1,256]{1,0:T(1,128)S(1)}, f32[1,256]{1,0:T(1,128)}, u32[]{:S(2)}) copy-start(f32[1,256]{1,0:T(1,128)} %get-tuple-element.18) | copy-start | bytes 3076

commit v2 on v1

--- a/solution.py
+++ b/solution.py
@@ -37,7 +37,7 @@
     w2_hbm,
     z_out,
     p_out,
-    u_out,
+    ut_out,
     e_out,
     gain_out,
     w1,
@@ -46,6 +46,7 @@
     p_keep,
     h_all,
     u_all,
+    ut,
     e_all,
     acc,
     f_send,
@@ -73,7 +74,7 @@
     gain_ssem,
     gain_rsem,
 ):
-    stages, parts, replicas = sizes
+    stages, parts, replicas, hop_width = sizes
     sec = lax.axis_index("pipe")
     me = lax.axis_index("mp")
     rep = lax.axis_index("dp")
@@ -81,6 +82,7 @@
     rows = h_all.shape[0]
     own = rows // parts
     width = full // parts
+    chunks = f_send.shape[1] // hop_width
     first = sec == 0
     last = sec == stages - 1
 
@@ -91,9 +93,9 @@
             pltpu.make_async_copy(w2_hbm.at[pl.ds(start, tile), :], w2.at[i], w2_sem.at[i]),
         )
 
-    for i in range(tiles):
-        for copy in w_copies(i):
-            copy.start()
+    for which in range(2):
+        for i in range(tiles):
+            w_copies(i)[which].start()
 
     barrier = pltpu.get_barrier_semaphore()
     peers = []
@@ -136,25 +138,54 @@
             for j, part in others()
         ]
 
-    def row_copies(dst, which):
+    chips = parts // 2
+    chip, core = me // 2, lax.rem(me, 2)
+    mate = chip * 2 + 1 - core
+
+    def columns(q):
+        return pl.ds(pl.multiple_of(q * hop_width, hop_width), hop_width)
+
+    def block_rows(k):
+        block = lax.rem(chip + chips - k, chips) * 2 + core
+        return pl.ds(pl.multiple_of(block * own, own), own)
+
+    def chip_copy(ref, which, q, k):
+        part = ref.at[my_rows, columns(q)]
+        target = lax.rem(chip + k, chips) * 2 + core
+        return remote(
+            part, part, ag_ssem.at[which, q, k], ag_rsem.at[which, q, k], {"mp": target}
+        )
+
+    def mate_copy(ref, which, q, k):
+        part = ref.at[block_rows(k), columns(q)]
+        slot = chips + k
+        return remote(
+            part, part, ag_ssem.at[which, q, slot], ag_rsem.at[which, q, slot], {"mp": mate}
+        )
+
+    def gather(ref, which, hop):
+        for q in range(chunks):
+            hop(q).wait_recv()
+            for k in range(1, chips):
+                chip_copy(ref, which, q, k).start()
+            mate_copy(ref, which, q, 0).start()
+        for q in range(chunks):
+            for k in range(1, chips):
+                chip_copy(ref, which, q, k).wait_recv()
+                mate_copy(ref, which, q, k).start()
+        for q in range(chunks):
+            for k in range(1, chips):
+                chip_copy(ref, which, q, k).wait_send()
+            for k in range(chips):
+                mate_copy(ref, which, q, k).wait()
+
+    def sum_copies(src, dst, which, q):
         return [
             remote(
-                dst.at[my_rows, :],
-                dst.at[my_rows, :],
-                ag_ssem.at[which, j],
-                ag_rsem.at[which, j],
-                {"mp": part},
-            )
-            for j, part in others()
-        ]
-
-    def sum_copies(src, dst, which):
-        return [
-            remote(
-                src.at[pl.ds(pl.multiple_of(part * own, own), own), :],
-                dst.at[j],
-                rs_ssem.at[which, j],
-                rs_rsem.at[which, j],
+                src.at[pl.ds(pl.multiple_of(part * own, own), own), columns(q)],
+                dst.at[j, :, columns(q)],
+                rs_ssem.at[which, q, j],
+                rs_rsem.at[which, q, j],
                 {"mp": part},
             )
             for j, part in others()
@@ -180,23 +211,64 @@
         for copy in copies:
             copy.wait()
 
-    def forward_hop():
+    def forward_hop(q):
         return remote(
-            h_hop,
-            h_all.at[my_rows, :],
-            hop_sem.at[0],
-            hop_sem.at[1],
+            h_hop.at[:, columns(q)],
+            h_all.at[my_rows, columns(q)],
+            hop_sem.at[0, q],
+            hop_sem.at[1, q],
             {"pipe": lax.rem(sec + 1, stages)},
         )
 
-    def backward_hop():
+    def backward_hop(q):
         return remote(
-            g_hop,
-            e_all.at[0, my_rows, :],
-            hop_sem.at[2],
-            hop_sem.at[3],
+            g_hop.at[:, columns(q)],
+            e_all.at[0, my_rows, columns(q)],
+            hop_sem.at[2, q],
+            hop_sem.at[3, q],
             {"pipe": lax.rem(sec + stages - 1, stages)},
         )
+
+    step_width = math.gcd(tile, 256)
+    steps = tile // step_width
+
+    def staged(product, use):
+        held = product(0)
+        for s in range(1, steps):
+            ahead = product(s)
+            use(s - 1, held)
+            held = ahead
+        use(steps - 1, held)
+
+    def activate(d, i, scaled=False):
+        def product(s):
+            piece = w1[i, :, s * step_width : (s + 1) * step_width]
+            return jnp.dot(u_all[d], piece, preferred_element_type=jnp.float32)
+
+        def use(s, gate):
+            place = slice(s * step_width, (s + 1) * step_width)
+            output, slope = gelu_parts(gate)
+            z_keep[d, i, :, place] = output.astype(jnp.bfloat16)
+            if scaled:
+                slope = slope * p_keep[d, i, :, place].astype(jnp.float32)
+            p_keep[d, i, :, place] = slope.astype(jnp.bfloat16)
+
+        staged(product, use)
+
+    def pregrad(d, i, scaled=True):
+        def product(s):
+            piece = w2[i, s * step_width : (s + 1) * step_width, :]
+            return lax.dot_general(
+                e_all[d], piece, CONTRACT_LAST, preferred_element_type=jnp.float32
+            )
+
+        def use(s, inner):
+            place = slice(s * step_width, (s + 1) * step_width)
+            if scaled:
+                inner = inner * p_keep[d, i, :, place].astype(jnp.float32)
+            p_keep[d, i, :, place] = inner.astype(jnp.bfloat16)
+
+        staged(product, use)
 
     @pl.when(last)
     def _():
@@ -206,6 +278,11 @@
         finish(copies)
         start(replica_copies(e_all, 1))
 
+        @pl.loop(0, tiles)
+        def _(i):
+            w_copies(i)[1].wait()
+            pregrad(0, i, scaled=False)
+
     @pl.when(first)
     def _():
         copies = feature_copies(x_ref, h_all)
@@ -215,15 +292,11 @@
 
     @pl.when(jnp.logical_not(first))
     def _():
-        forward_hop().wait_recv()
-        copies = row_copies(h_all, 0)
-        start(copies)
-        finish(copies)
+        gather(h_all, 0, forward_hop)
 
     values = h_all[...].astype(jnp.float32)
     u_all[0] = (values * inverse_rms(values) * gain_ref[...]).astype(jnp.bfloat16)
     start(replica_copies(u_all, 0))
-    acc[...] = jnp.zeros_like(acc)
 
     def z_copy(d, i):
         return pltpu.make_async_copy(
@@ -239,43 +312,49 @@
             p_sem.at[d, i],
         )
 
-    def activate(d, i):
-        gate = jnp.dot(u_all[d], w1[i], preferred_element_type=jnp.float32)
-        output, slope = gelu_parts(gate)
-        output = output.astype(jnp.bfloat16)
-        z_keep[d, i] = output
-        p_keep[d, i] = slope.astype(jnp.bfloat16)
-        return output
-
-    def pregrad(d, i):
-        inner = lax.dot_general(
-            e_all[d], w2[i], CONTRACT_LAST, preferred_element_type=jnp.float32
-        )
-        grad = (inner * p_keep[d, i].astype(jnp.float32)).astype(jnp.bfloat16)
-        p_keep[d, i] = grad
-        return grad
-
-    @pl.loop(0, tiles)
-    def _(i):
-        for copy in w_copies(i):
+    @pl.when(last)
+    def _():
+        @pl.loop(0, tiles)
+        def _(i):
+            w_copies(i)[0].wait()
+            activate(0, i, scaled=True)
+            p_copy(0, i).start()
+
+    def pass_on(q):
+        total = h_all[my_rows, columns(q)].astype(jnp.float32) + acc[my_rows, columns(q)]
+        for j, copy in enumerate(sum_copies(f_send, f_recv, 0, q)):
             copy.wait()
-        output = activate(0, i)
-
-        @pl.when(jnp.logical_not(last))
-        def _():
-            acc[...] += jnp.dot(output, w2[i], preferred_element_type=jnp.float32)
+            total += f_recv[j + 1, :, columns(q)].astype(jnp.float32)
+        h_hop[:, columns(q)] = total.astype(jnp.bfloat16)
+        forward_hop(q).start()
 
     @pl.when(jnp.logical_not(last))
     def _():
-        f_send[...] = acc[...].astype(jnp.bfloat16)
-        copies = sum_copies(f_send, f_recv, 0)
-        start(copies)
-        total = h_all[my_rows, :].astype(jnp.float32) + acc[my_rows, :]
-        for j, copy in enumerate(copies):
-            copy.wait()
-            total += f_recv[j + 1].astype(jnp.float32)
-        h_hop[...] = total.astype(jnp.bfloat16)
-        forward_hop().start()
+        @pl.loop(0, tiles)
+        def _(i):
+            w_copies(i)[0].wait()
+            activate(0, i)
+
+        @pl.loop(0, tiles)
+        def _(i):
+            w_copies(i)[1].wait()
+
+        @pl.loop(0, chunks)
+        def _(q):
+            total = jnp.zeros((rows, hop_width), jnp.float32)
+            for i in range(tiles):
+                total += jnp.dot(
+                    z_keep[0, i], w2[i, :, columns(q)], preferred_element_type=jnp.float32
+                )
+            acc[:, columns(q)] = total
+            f_send[:, columns(q)] = total.astype(jnp.bfloat16)
+            start(sum_copies(f_send, f_recv, 0, q))
+
+            @pl.when(q > 0)
+            def _():
+                pass_on(q - 1)
+
+        pass_on(chunks - 1)
 
     @pl.loop(0, tiles)
     def _(i):
@@ -290,45 +369,58 @@
                 activate(d, i)
                 z_copy(d, i).start()
 
+        half = full // replicas
+        kept = pl.ds(pl.multiple_of(rep * half, half), half)
+        for d in range(replicas):
+            flipped = u_all[d, :, kept].astype(jnp.float32).T
+            ut[:, d * rows : (d + 1) * rows] = flipped.astype(jnp.bfloat16)
+        pltpu.make_async_copy(ut, ut_out, out_sem.at[0, 0]).start()
+
     @pl.when(jnp.logical_not(last))
     def _():
         replica_forward()
-        forward_hop().wait_send()
-        backward_hop().wait_recv()
-        copies = row_copies(e_all.at[0], 1)
-        start(copies)
-        finish(copies)
+        for q in range(chunks):
+            forward_hop(q).wait_send()
+        gather(e_all.at[0], 1, backward_hop)
         start(replica_copies(e_all, 1))
 
-    acc[...] = jnp.zeros_like(acc)
-
-    @pl.loop(0, tiles)
-    def _(i):
-        grad = pregrad(0, i)
-        acc[...] += lax.dot_general(
-            grad, w1[i], CONTRACT_LAST, preferred_element_type=jnp.float32
-        )
-        p_copy(0, i).start()
+        @pl.loop(0, tiles)
+        def _(i):
+            pregrad(0, i)
+            p_copy(0, i).start()
+
+    @pl.loop(0, chunks)
+    def _(q):
+        total = jnp.zeros((rows, hop_width), jnp.float32)
+        for i in range(tiles):
+            total += lax.dot_general(
+                p_keep[0, i], w1[i, columns(q), :], CONTRACT_LAST, preferred_element_type=jnp.float32
+            )
+        acc[:, columns(q)] = total
+
+        @pl.when(jnp.logical_not(first))
+        def _():
+            b_send[:, columns(q)] = total.astype(jnp.bfloat16)
+            start(sum_copies(b_send, b_recv, 1, q))
 
     @pl.when(jnp.logical_not(first))
     def _():
-        b_send[...] = acc[...].astype(jnp.bfloat16)
-        copies = sum_copies(b_send, b_recv, 1)
-        start(copies)
         mine = h_all[my_rows, :].astype(jnp.float32)
         scale = inverse_rms(mine)
         unit = mine * scale
         total = acc[my_rows, :]
-        for j, copy in enumerate(copies):
-            copy.wait()
-            total += b_recv[j + 1].astype(jnp.float32)
+        for q in range(chunks):
+            finish(sum_copies(b_send, b_recv, 1, q))
+        for j in range(1, parts):
+            total += b_recv[j].astype(jnp.float32)
         scaled = total * gain_ref[...]
         row_dot = jnp.sum(scaled * unit, axis=1, keepdims=True)
         previous = e_all[0, my_rows, :].astype(jnp.float32) + scale * (
             scaled - unit * (row_dot / full)
         )
         g_hop[...] = previous.astype(jnp.bfloat16)
-        backward_hop().start()
+        for q in range(chunks):
+            backward_hop(q).start()
 
     values = h_all[...].astype(jnp.float32)
     terms = acc[...] * (values * inverse_rms(values))
@@ -360,9 +452,9 @@
     outs = []
     for d in range(replicas):
         place = pl.ds(d * rows, rows)
-        outs.append(pltpu.make_async_copy(u_all.at[d], u_out.at[place, :], out_sem.at[0, d]))
         outs.append(pltpu.make_async_copy(e_all.at[d], e_out.at[place, :], out_sem.at[1, d]))
     start(outs)
+    outs.append(pltpu.make_async_copy(ut, ut_out, out_sem.at[0, 0]))
     total = gain_part[:, my_cols]
     for (d, j, _, _), copy in zip(peers, gain_copies):
         copy.wait()
@@ -380,7 +472,8 @@
 
     @pl.when(jnp.logical_not(first))
     def _():
-        backward_hop().wait_send()
+        for q in range(chunks):
+            backward_hop(q).wait_send()
 
 
 def shards(inputs, cotangent, gain, weight_in, weight_out):
@@ -395,17 +488,19 @@
     tiles = hidden // tile
     own = rows // parts
     half = full // replicas
+    hop_width = math.gcd(full, 256)
+    chunks = full // hop_width
     bf16, f32 = jnp.bfloat16, jnp.float32
     vmem = pl.BlockSpec(memory_space=pltpu.VMEM)
     anywhere = pl.BlockSpec(memory_space=pl.ANY)
     dma = pltpu.SemaphoreType.DMA
-    z_all, p_all, u_all, e_all, gain_total = pl.pallas_call(
-        functools.partial(relay, (stages, parts, replicas)),
+    z_all, p_all, u_flip, e_all, gain_total = pl.pallas_call(
+        functools.partial(relay, (stages, parts, replicas, hop_width)),
         name="relay",
         out_shape=(
             jax.ShapeDtypeStruct((replicas * rows, hidden), bf16),
             jax.ShapeDtypeStruct((replicas * rows, hidden), bf16),
-            jax.ShapeDtypeStruct((replicas * rows, full), bf16),
+            jax.ShapeDtypeStruct((half, replicas * rows), bf16),
             jax.ShapeDtypeStruct((replicas * rows, full), bf16),
             jax.ShapeDtypeStruct((1, width), f32),
         ),
@@ -418,6 +513,7 @@
             pltpu.VMEM((replicas, tiles, rows, tile), bf16),
             pltpu.VMEM((rows, full), bf16),
             pltpu.VMEM((replicas, rows, full), bf16),
+            pltpu.VMEM((half, replicas * rows), bf16),
             pltpu.VMEM((replicas, rows, full), bf16),
             pltpu.VMEM((rows, full), f32),
             pltpu.VMEM((rows, full), bf16),
@@ -435,13 +531,13 @@
             dma((2, replicas)),
             dma((parts,)),
             dma((parts,)),
-            dma((4,)),
-            dma((2, parts)),
-            dma((2, parts)),
+            dma((4, chunks)),
+            dma((2, chunks, parts)),
+            dma((2, chunks, parts)),
             dma((2, replicas)),
             dma((2, replicas)),
-            dma((2, parts)),
-            dma((2, parts)),
+            dma((2, chunks, parts)),
+            dma((2, chunks, parts)),
             dma((replicas * parts,)),
             dma((replicas * parts,)),
         ],
@@ -456,9 +552,8 @@
         weight_out[0],
     )
     begin = lax.axis_index("dp") * half
-    u_cols = lax.dynamic_slice_in_dim(u_all, begin, half, 1)
     e_cols = lax.dynamic_slice_in_dim(e_all, begin, half, 1)
-    grad_first = lax.dot_general(u_cols, p_all, CONTRACT_FIRST, preferred_element_type=f32)
+    grad_first = jnp.dot(u_flip, p_all, preferred_element_type=f32)
     grad_second = lax.dot_general(z_all, e_cols, CONTRACT_FIRST, preferred_element_type=f32)
     return (grad_first.astype(bf16)[None], grad_second.astype(bf16)[None], gain_total)
 

time: 248 us -> 214 us (0.86)
  Pallas kernels: 226 us -> 191 us
  matrix products: 18.6 us -> 21.8 us
    pallas_call x1, Pallas kernels: 226 us -> 191 us  [shards(): pl.pallas_call(functools.partial(relay, (stages, parts, replicas, hop_wid...]
    dot_general x1, matrix products: 6.98 us -> 10.2 us  [shards(): lax.dot_general(z_all, e_cols, CONTRACT_FIRST, preferred_element_type=f32)]
where the time goes in v2:
time: 214 us
  Pallas kernels  191 us (89%)
  matrix products  21.8 us (10%)
    pallas_call x1, Pallas kernels, shards(): pl.pallas_call(functools.partial(relay, (stages, parts, replicas, hop_wid...  191 us
    dot_general x1, matrix products, shards(): grad_first = jnp.dot(u_flip, p_all, preferred_element_type=f32)  11.6 us
    dot_general x1, matrix products, shards(): lax.dot_general(z_all, e_cols, CONTRACT_FIRST, preferred_element_type=f32)  10.2 us

profile of v2, /device:TPU:0, one launch (start us, length us, event | category | flops | bytes accessed | tf_op | source)
XLA Modules:
  0.0 213.6 jit_solution(8763880465068825756)
XLA Ops:
  0.6 190.5 %relay.1 = (bf16[512,8192]{1,0:T(8,128)(2,1)}, bf16[512,8192]{1,0:T(8,128)(2,1)}, bf16[512,512]{1,0:T(8,128)(2,1)}, bf16[512,1024]{1,0:T(8,128)(2,1)}, f32[1,256]{1,0:T(1,128)}) custom-call(bf16[256,256]{1,0:T(8,128)(2,1)} %bitcast.13, bf16[256,256]{1,0:T(8,128)(2,1)} %bitcast.14, f32[1,1024]{1,0:T(1,128)} %gain_ref.1, bf16[1024,8192]{1,0:T(8,128)(2,1)} %bitcast.11, ...), custom_call_target="tpu_custom_call" | custom-call | tf_op jit(solution)/shard_map/relay/pallas_call | solution.py:497
  191.2 0.0 copy-start.1
  191.2 11.6 %fusion = bf16[1,512,8192]{2,1,0:T(8,128)(2,1)} fusion(bf16[512,512]{1,0:T(8,128)(2,1)} %get-tuple-element.8, bf16[512,8192]{1,0:T(8,128)(2,1)} %get-tuple-element.9), kind=kOutput, calls=%fused_computation.2 | convolution fusion | flops 4299161600 | bytes 17301504 | tf_op jit(solution)/shard_map/dot_general | solution.py:556
  202.7 0.0 copy-done.1
  202.7 0.0 copy-start
  202.7 10.2 %fusion.1 = bf16[1,8192,512]{2,1,0:T(8,128)(2,1)} fusion(bf16[512,8192]{1,0:T(8,128)(2,1)} %get-tuple-element.10, bf16[512,1024]{1,0:T(8,128)(2,1)S(1)} %copy-done.1, s32[]{:T(128)S(6)} %select_n.3), kind=kOutput, calls=%fused_computation.3 | convolution fusion | flops 4299161600 | bytes 17301508 | tf_op jit(solution)/shard_map/dot_general | solution.py:557
  213.0 0.0 copy-done
  213.0 0.6 copy.9
Async XLA Ops:
  191.2 11.6 %copy-start.1 = (bf16[512,1024]{1,0:T(8,128)(2,1)S(1)}, bf16[512,1024]{1,0:T(8,128)(2,1)}, u32[]{:S(2)}) copy-start(bf16[512,1024]{1,0:T(8,128)(2,1)} %get-tuple-element.11) | copy-start | bytes 3145732
  202.7 10.3 %copy-start = (f32[1,256]{1,0:T(1,128)S(1)}, f32[1,256]{1,0:T(1,128)}, u32[]{:S(2)}) copy-start(f32[1,256]{1,0:T(1,128)} %get-tuple-element.18) | copy-start | bytes 3076

commit v3 on v2

--- a/solution.py
+++ b/solution.py
@@ -119,6 +119,9 @@
     my_rows = pl.ds(pl.multiple_of(me * own, own), own)
     my_cols = pl.ds(pl.multiple_of(me * width, width), width)
 
+    half = full // replicas
+    kept = pl.ds(pl.multiple_of(rep * half, half), half)
+
     def remote(src, dst, ssem, rsem, where):
         return pltpu.make_async_remote_copy(
             src_ref=src,
@@ -132,12 +135,6 @@
     def others():
         return [(j, lax.rem(me + j, parts)) for j in range(1, parts)]
 
-    def feature_copies(src, dst):
-        return [
-            remote(src, dst.at[:, my_cols], x_ssem.at[j], x_rsem.at[j], {"mp": part})
-            for j, part in others()
-        ]
-
     chips = parts // 2
     chip, core = me // 2, lax.rem(me, 2)
     mate = chip * 2 + 1 - core
@@ -162,6 +159,34 @@
         return remote(
             part, part, ag_ssem.at[which, q, slot], ag_rsem.at[which, q, slot], {"mp": mate}
         )
+
+    def gather_features(src, dst):
+        def cols(k):
+            block = lax.rem(chip + chips - k, chips) * 2 + core
+            return pl.ds(pl.multiple_of(block * width, width), width)
+
+        def across(k):
+            target = lax.rem(chip + k, chips) * 2 + core
+            return remote(src, dst.at[:, my_cols], x_ssem.at[k], x_rsem.at[k], {"mp": target})
+
+        def beside(k):
+            part = dst.at[:, cols(k)]
+            slot = chips + k
+            return remote(
+                src if k == 0 else part, part, x_ssem.at[slot], x_rsem.at[slot], {"mp": mate}
+            )
+
+        for k in range(1, chips):
+            across(k).start()
+        beside(0).start()
+        dst[:, my_cols] = src[...]
+        for k in range(1, chips):
+            across(k).wait_recv()
+            beside(k).start()
+        for k in range(1, chips):
+            across(k).wait_send()
+        for k in range(chips):
+            beside(k).wait()
 
     def gather(ref, which, hop):
         for q in range(chunks):
@@ -272,10 +297,7 @@
 
     @pl.when(last)
     def _():
-        copies = feature_copies(cot_ref, e_all.at[0])
-        start(copies)
-        e_all[0, :, my_cols] = cot_ref[...]
-        finish(copies)
+        gather_features(cot_ref, e_all.at[0])
         start(replica_copies(e_all, 1))
 
         @pl.loop(0, tiles)
@@ -285,10 +307,7 @@
 
     @pl.when(first)
     def _():
-        copies = feature_copies(x_ref, h_all)
-        start(copies)
-        h_all[:, my_cols] = x_ref[...]
-        finish(copies)
+        gather_features(x_ref, h_all)
 
     @pl.when(jnp.logical_not(first))
     def _():
@@ -369,8 +388,6 @@
                 activate(d, i)
                 z_copy(d, i).start()
 
-        half = full // replicas
-        kept = pl.ds(pl.multiple_of(rep * half, half), half)
         for d in range(replicas):
             flipped = u_all[d, :, kept].astype(jnp.float32).T
             ut[:, d * rows : (d + 1) * rows] = flipped.astype(jnp.bfloat16)
@@ -452,7 +469,7 @@
     outs = []
     for d in range(replicas):
         place = pl.ds(d * rows, rows)
-        outs.append(pltpu.make_async_copy(e_all.at[d], e_out.at[place, :], out_sem.at[1, d]))
+        outs.append(pltpu.make_async_copy(e_all.at[d, :, kept], e_out.at[place, :], out_sem.at[1, d]))
     start(outs)
     outs.append(pltpu.make_async_copy(ut, ut_out, out_sem.at[0, 0]))
     total = gain_part[:, my_cols]
@@ -474,6 +491,15 @@
     def _():
         for q in range(chunks):
             backward_hop(q).wait_send()
+
+
+def weight_grads(u_ref, e_ref, p_ref, z_ref, in_ref, out_ref):
+    in_ref[...] = jnp.dot(
+        u_ref[...], p_ref[...], preferred_element_type=jnp.float32
+    ).astype(in_ref.dtype)
+    out_ref[...] = lax.dot_general(
+        z_ref[...], e_ref[...], CONTRACT_FIRST, preferred_element_type=jnp.float32
+    ).astype(out_ref.dtype)
 
 
 def shards(inputs, cotangent, gain, weight_in, weight_out):
@@ -494,14 +520,14 @@
     vmem = pl.BlockSpec(memory_space=pltpu.VMEM)
     anywhere = pl.BlockSpec(memory_space=pl.ANY)
     dma = pltpu.SemaphoreType.DMA
-    z_all, p_all, u_flip, e_all, gain_total = pl.pallas_call(
+    z_all, p_all, u_flip, e_cols, gain_total = pl.pallas_call(
         functools.partial(relay, (stages, parts, replicas, hop_width)),
         name="relay",
         out_shape=(
             jax.ShapeDtypeStruct((replicas * rows, hidden), bf16),
             jax.ShapeDtypeStruct((replicas * rows, hidden), bf16),
             jax.ShapeDtypeStruct((half, replicas * rows), bf16),
-            jax.ShapeDtypeStruct((replicas * rows, full), bf16),
+            jax.ShapeDtypeStruct((replicas * rows, half), bf16),
             jax.ShapeDtypeStruct((1, width), f32),
         ),
         in_specs=[vmem, vmem, vmem, anywhere, anywhere],
@@ -551,11 +577,28 @@
         weight_in[0],
         weight_out[0],
     )
-    begin = lax.axis_index("dp") * half
-    e_cols = lax.dynamic_slice_in_dim(e_all, begin, half, 1)
-    grad_first = jnp.dot(u_flip, p_all, preferred_element_type=f32)
-    grad_second = lax.dot_general(z_all, e_cols, CONTRACT_FIRST, preferred_element_type=f32)
-    return (grad_first.astype(bf16)[None], grad_second.astype(bf16)[None], gain_total)
+    count = replicas * rows
+    grad_first, grad_second = pl.pallas_call(
+        weight_grads,
+        name="weight_grads",
+        grid=(tiles,),
+        out_shape=(
+            jax.ShapeDtypeStruct((full // replicas, hidden), bf16),
+            jax.ShapeDtypeStruct((hidden, half), bf16),
+        ),
+        in_specs=[
+            vmem,
+            vmem,
+            pl.BlockSpec((count, tile), lambda i: (0, i)),
+            pl.BlockSpec((count, tile), lambda i: (0, i)),
+        ],
+        out_specs=(
+            pl.BlockSpec((half, tile), lambda i: (0, i)),
+            pl.BlockSpec((tile, half), lambda i: (i, 0)),
+        ),
+        compiler_params=pltpu.CompilerParams(vmem_limit_bytes=67043328),
+    )(u_flip, e_cols, p_all, z_all)
+    return (grad_first[None], grad_second[None], gain_total)
 
 
 def solution(mesh):

time: 214 us -> 208 us (0.972)
  matrix products: 21.8 us -> 0 us
  Pallas kernels: 191 us -> 206 us
    dot_general x2 -> x0, matrix products: 21.8 us -> none  [the longest x1 11.6 us: shards(): grad_first = jnp.dot(u_flip, p_all, preferred_element_type=f32)]
    pallas_call x0 -> x1, Pallas kernels: none -> 17 us  [shards(): pl.pallas_call(weight_grads, name='weight_grads', grid=(tiles,), out_shap...]
where the time goes in v3:
time: 208 us
  Pallas kernels  206 us (99%)
    pallas_call x1, Pallas kernels, shards(): pl.pallas_call(functools.partial(relay, (stages, parts, replicas, hop_wid...  189 us
    pallas_call x1, Pallas kernels, shards(): pl.pallas_call(weight_grads, name='weight_grads', grid=(tiles,), out_shap...  17 us

profile of v3, /device:TPU:0, one launch (start us, length us, event | category | flops | bytes accessed | tf_op | source)
XLA Modules:
  0.0 208.2 jit_solution(15794234005323691067)
XLA Ops:
  0.6 189.4 %relay.1 = (bf16[512,8192]{1,0:T(8,128)(2,1)}, bf16[512,8192]{1,0:T(8,128)(2,1)}, bf16[512,512]{1,0:T(8,128)(2,1)}, bf16[512,512]{1,0:T(8,128)(2,1)}, f32[1,256]{1,0:T(1,128)}) custom-call(bf16[256,256]{1,0:T(8,128)(2,1)} %bitcast.8, bf16[256,256]{1,0:T(8,128)(2,1)} %bitcast.9, f32[1,1024]{1,0:T(1,128)} %gain_ref.1, bf16[1024,8192]{1,0:T(8,128)(2,1)} %bitcast.6, ...), custom_call_target="tpu_custom_call" | custom-call | tf_op jit(solution)/shard_map/relay/pallas_call | solution.py:523
  190.1 17.0 %weight_grads.1 = (bf16[512,8192]{1,0:T(8,128)(2,1)}, bf16[8192,512]{1,0:T(8,128)(2,1)}) custom-call(bf16[512,512]{1,0:T(8,128)(2,1)} %get-tuple-element.10.u_ref, bf16[512,512]{1,0:T(8,128)(2,1)} %get-tuple-element.11.e_ref, bf16[512,8192]{1,0:T(8,128)(2,1)} %get-tuple-element.12.p_ref, bf16[512,8192]{1,0:T(8,128)(2,1)} %get-tuple-element.13.z_ref), custom_call_target="tpu_custom_call" | custom-call | tf_op jit(solution)/shard_map/weight_grads/pallas_call | solution.py:581
  207.0 1.2 copy.9
